TPU v7x, 512 devices: a whole 4x4x16 slice. The times are simulated.
512 devices in a mesh: af: 8 (over x, z_hi), vert: 64 (over y, z_lo, core).
Axes of the slice: x: 4, y: 4, z: 16 (z_hi: 2, z_lo: 8; z = z_hi * 8 + z_lo), core: 2. Of those that a mesh axis runs over, the one named last changes fastest.
Arguments:
- signals: bfloat16 [1000, 16384], P('af', 'vert'), may hold values from -2000 to 2000
- basis: bfloat16 [10, 1000], P(None, 'af'), may hold values from -0.1875 to 0.1875
- atoms: float32 [10, 262144], P(None, ('af', 'vert')), may hold values from -6 to 6
- params: float32 [3, 262144], P(None, ('af', 'vert')), may hold values from -1.5 to 1.5
Outputs:
- coefficients: float32 [10, 16384], P(None, 'vert')
- maps: float32 [3, 16384], P(None, 'vert')
All inputs are finite; a program needn't handle non-finite values.
Results may differ from a plain program's by a relative error of at most 0.0003.
Values sent between devices are 32-bit elements; how exact they have to be, the bound alone decides.
No kernel may reach another device: no remote copies, remote signals or barrier semaphores. Data moves between devices by JAX's collectives and lax.ppermute only.
A program may use at most 64 MiB of HBM per device.

v0:
```python
import math
import jax
import jax.numpy as jnp
from jax import lax
from jax.sharding import PartitionSpec as P

score_scale = 1.5


def fold_block(running, coefficients, atom_piece, param_piece):
    run_peak, run_total, run_weighted = running
    scores = score_scale * lax.dot_general(
        coefficients,
        atom_piece,
        (((0,), (0,)), ((), ())),
        precision=lax.Precision.HIGHEST,
        preferred_element_type=jnp.float32,
    )
    new_peak = jnp.maximum(run_peak, jnp.max(scores, axis=1))
    weights = jnp.exp(scores - new_peak[:, None])
    factor = jnp.exp(run_peak - new_peak)
    run_total = run_total * factor + jnp.sum(weights, axis=1)
    run_weighted = run_weighted * factor[None, :] + lax.dot_general(
        param_piece,
        weights,
        (((1,), (1,)), ((), ())),
        precision=lax.Precision.HIGHEST,
        preferred_element_type=jnp.float32,
    )
    return (new_peak, run_total, run_weighted)


def make_folder(coefficients, running, pieces):
    atom_piece, param_piece = pieces
    piece_width = atom_piece.shape[1]
    block_size = math.gcd(piece_width, 2048)
    block_count = piece_width // block_size
    atom_blocks = atom_piece.reshape(atom_piece.shape[0], block_count, block_size).transpose(
        1, 0, 2
    )
    param_blocks = param_piece.reshape(3, block_count, block_size).transpose(1, 0, 2)

    def step(state, blocks):
        return (fold_block(state, coefficients, blocks[0], blocks[1]), None)

    result, unused = lax.scan(step, running, (atom_blocks, param_blocks))
    return result


def start_state(voxels):
    return (
        jnp.full((voxels,), -1e30, jnp.float32),
        jnp.zeros((voxels,), jnp.float32),
        jnp.zeros((3, voxels), jnp.float32),
    )


def on_device(signals, basis, atoms, params):
    partial_sums = jnp.dot(basis, signals, preferred_element_type=jnp.float32)
    coefficients = lax.psum(partial_sums, "af")
    run_peak, run_total, run_weighted = make_folder(
        coefficients,
        start_state(coefficients.shape[1]),
        (
            lax.all_gather(atoms, "vert", axis=1, tiled=True),
            lax.all_gather(params, "vert", axis=1, tiled=True),
        ),
    )
    global_peak = lax.pmax(run_peak, "af")
    factor = jnp.exp(run_peak - global_peak)
    run_total, run_weighted = lax.psum((run_total * factor, run_weighted * factor[None, :]), "af")
    maps = run_weighted / run_total[None, :]
    return (coefficients, maps)


def solution(mesh):
    placed = (P("af", "vert"), P(None, "af"), P(None, ("af", "vert")), P(None, ("af", "vert")))
    return jax.shard_map(
        on_device,
        mesh=mesh,
        in_specs=placed,
        out_specs=(P(None, "vert"), P(None, "vert")),
        check_vma=False,
    )
```

profile of v0, /device:TPU:2, one launch (start us, length us, event | category | flops | bytes accessed | tf_op | source)
XLA Modules:
  0.0 352.7 jit_solution(9641014140261085518)
XLA Ops:
  8.8 79.5 %psum.21 = f32[10,256]{1,0:T(8,128)S(1)} all-reduce(f32[10,256]{1,0:T(8,128)S(1)} %fusion.11), channel_id=1, replica_groups=mesh['af'=8,'vert'=64] {'af'}, use_global_device_ids=true, to_apply=%region_0.0 | all-reduce | flops 2560 | bytes 20480 | tf_op jit(solution)/shard_map/psum | solution.py:60
  88.4 120.6 %all_gather.7 = f32[3,32768]{1,0:T(4,128)S(1)} all-gather(f32[3,512]{1,0:T(4,128)} %param.9), channel_id=1, replica_groups=mesh['af'=8,'vert'=64] {'vert'}, dimensions={1}, use_global_device_ids=true | all-gather | bytes 399360 | tf_op jit(solution)/shard_map/all_gather | solution.py:66
  209.0 2.8 copy.8
  211.9 55.3 %while.15 = (s32[]{:T(128)}, f32[256]{0:T(256)S(1)}, f32[256]{0:T(256)S(1)}, f32[3,256]{1,0:T(4,128)S(1)}, f32[16,10,2048]{2,0,1:T(8,128)S(1)}, /*index=5*/f32[1...) while((s32[]{:T(128)}, f32[256]{0:T(256)S(1)}, f32[256]{0:T(256)S(1)}, ...), condition=%wide.region_4.5_spmd.clone, body=%wide.region_1.4_spmd.clone.sunk | while | flops 84413952 | bytes 6603897 | solution.py:46
  212.0 1.9 fusion.24
  215.5 1.9 fusion.24
  217.7 1.1 fusion.28
  218.9 1.9 fusion.24
  221.2 1.1 fusion.28
  222.4 1.9 fusion.24
  224.6 1.1 fusion.28
  225.9 1.9 fusion.24
  228.1 1.1 fusion.28
  229.3 1.9 fusion.24
  231.6 1.1 fusion.28
  232.8 1.9 fusion.24
  235.0 1.1 fusion.28
  236.2 1.9 fusion.24
  238.5 1.1 fusion.28
  239.7 1.9 fusion.24
  241.9 1.1 fusion.28
  243.1 1.9 fusion.24
  245.4 1.1 fusion.28
  246.6 1.9 fusion.24
  248.8 1.1 fusion.28
  250.0 1.9 fusion.24
  253.5 1.9 fusion.24
  257.0 1.9 fusion.24
  260.4 1.9 fusion.24
  263.9 1.9 fusion.24
  267.2 33.7 %pmax.7 = f32[256]{0:T(256)S(1)} all-reduce(f32[256]{0:T(256)S(1)} %get-tuple-element.42), channel_id=1, replica_groups=mesh['af'=8,'vert'=64] {'af'}, use_global_device_ids=true, to_apply=%region_5.6 | all-reduce | flops 256 | bytes 2048 | tf_op jit(solution)/shard_map/pmax | solution.py:69
  300.9 44.3 %all-reduce = (f32[3,256]{1,0:T(4,128)S(1)}, f32[256]{0:T(256)S(1)}) all-reduce(f32[3,256]{1,0:T(4,128)S(1)} %broadcast_multiply_fusion, f32[256]{0:T(256)S(1)} %get-tuple-element.93), channel_id=1, replica_groups=mesh['af'=8,'vert'=64] {'af'}, use_global_device_ids=true, to_apply=%region_6.7 | all-reduce | flops 1024 | bytes 8192 | tf_op jit(solution)/shard_map/psum | solution.py:71
  (101 shorter events, 16.2 us)
Async XLA Ops:
  7.2 0.8 copy-start
  7.2 201.8 %all-gather.2.cloned.1.call-start = ((), (), s32[]{:S(2)}) async-start(), calls=%async_computation | async-start | bytes 2129920 | tf_op jit(solution)/shard_map/all_gather | solution.py:65
  267.2 78.6 %copy-start.1 = (f32[10,256]{1,0:T(8,128)}, f32[10,256]{1,0:T(8,128)S(1)}, u32[]{:S(2)}) copy-start(f32[10,256]{1,0:T(8,128)S(1)} %get-tuple-element.177) | copy-start | bytes 30724
Sparse Core Ops, SparseCore 0:
  10.2 125.4 all-gather.1
where the time goes:
time: 353 us
  blocking collectives  278 us (79%)
  matrix products  48.2 us (14%)
  between operations  14.1 us (4%)
  other arithmetic  6.72 us (2%)
  local copies, waits for them, and re-layouts  4.12 us (1%)
    all_gather x1, blocking collectives, on_device(): lax.all_gather(params, 'vert', axis=1, tiled=True)  121 us
    psum x1, blocking collectives, on_device(): coefficients = lax.psum(partial_sums, 'af')  79.5 us
    psum x1, blocking collectives, on_device(): lax.psum((run_total * factor, run_weighted * factor[None, :]), 'af')  44.3 us
    pmax x1, blocking collectives, on_device(): global_peak = lax.pmax(run_peak, 'af')  33.7 us
    dot_general x16, matrix products, fold_block(): lax.dot_general(coefficients, atom_piece, (((0,), (0,)), ((), ())), preci...  29.7 us
    dot_general x16, matrix products, fold_block(): lax.dot_general(param_piece, weights, (((1,), (1,)), ((), ())), precision...  17.7 us
  transfers between devices with their start and end apart: 1, of which 0 were waited for; matrix products, arithmetic and copies ran while one was open for 0% of the time, Pallas kernels for 0%

commit v1 on v0

--- a/solution.py
+++ b/solution.py
@@ -57,7 +57,7 @@
 
 def on_device(signals, basis, atoms, params):
     partial_sums = jnp.dot(basis, signals, preferred_element_type=jnp.float32)
-    coefficients = lax.psum(partial_sums, "af")
+    coefficients = jnp.sum(lax.all_gather(partial_sums, "af"), axis=0)
     run_peak, run_total, run_weighted = make_folder(
         coefficients,
         start_state(coefficients.shape[1]),

time: 353 us -> 342 us (0.969)
  blocking collectives: 278 us -> 268 us
    psum x1 -> x0, blocking collectives: 79.5 us -> none  [on_device(): coefficients = lax.psum(partial_sums, 'af')]
    all_gather x0 -> x1, blocking collectives: none -> 66.6 us  [on_device(): coefficients = jnp.sum(lax.all_gather(partial_sums, 'af'), axis=0)]
    pmax x1, blocking collectives: 33.7 us -> 42.2 us  [on_device(): global_peak = lax.pmax(run_peak, 'af')]
    psum x1, blocking collectives: 44.3 us -> 36 us  [on_device(): lax.psum((run_total * factor, run_weighted * factor[None, :]), 'af')]
where the time goes in v1:
time: 342 us
  blocking collectives  268 us (78%)
  matrix products  48.2 us (14%)
  between operations  14.1 us (4%)
  other arithmetic  6.73 us (2%)
  local copies, waits for them, and re-layouts  4.12 us (1%)
    all_gather x1, blocking collectives, on_device(): lax.all_gather(params, 'vert', axis=1, tiled=True)  123 us
    all_gather x1, blocking collectives, on_device(): coefficients = jnp.sum(lax.all_gather(partial_sums, 'af'), axis=0)  66.6 us
    pmax x1, blocking collectives, on_device(): global_peak = lax.pmax(run_peak, 'af')  42.2 us
    psum x1, blocking collectives, on_device(): lax.psum((run_total * factor, run_weighted * factor[None, :]), 'af')  36 us
    dot_general x16, matrix products, fold_block(): lax.dot_general(coefficients, atom_piece, (((0,), (0,)), ((), ())), preci...  29.7 us
    dot_general x16, matrix products, fold_block(): lax.dot_general(param_piece, weights, (((1,), (1,)), ((), ())), precision...  17.7 us
  transfers between devices with their start and end apart: 1, of which 0 were waited for; matrix products, arithmetic and copies ran while one was open for 0% of the time, Pallas kernels for 0%

profile of v1, /device:TPU:2, one launch (start us, length us, event | category | flops | bytes accessed | tf_op | source)
XLA Modules:
  0.0 342.2 jit_solution(15187238834506961707)
XLA Ops:
  8.8 66.6 %all-gather.1 = f32[8,10,256]{2,1,0:T(8,128)S(1)} all-gather(f32[1,10,256]{2,1,0:T(8,128)S(1)} %convolution_bitcast_fusion), channel_id=2, replica_groups=mesh['af'=8,'vert'=64] {'af'}, dimensions={0}, use_global_device_ids=true | all-gather | bytes 92160 | tf_op jit(solution)/shard_map/all_gather | solution.py:60
  75.5 122.9 %all_gather.15 = f32[3,32768]{1,0:T(4,128)S(1)} all-gather(f32[3,512]{1,0:T(4,128)} %param.9), channel_id=1, replica_groups=mesh['af'=8,'vert'=64] {'vert'}, dimensions={1}, use_global_device_ids=true | all-gather | bytes 399360 | tf_op jit(solution)/shard_map/all_gather | solution.py:66
  198.4 2.8 copy.9
  201.3 55.2 %while.15 = (s32[]{:T(128)}, f32[256]{0:T(256)S(1)}, f32[256]{0:T(256)S(1)}, f32[3,256]{1,0:T(4,128)S(1)}, f32[16,10,2048]{2,0,1:T(8,128)S(1)}, /*index=5*/f32[1...) while((s32[]{:T(128)}, f32[256]{0:T(256)S(1)}, f32[256]{0:T(256)S(1)}, ...), condition=%wide.region_4.5_spmd.clone, body=%wide.region_1.4_spmd.clone.sunk | while | flops 84413952 | bytes 6603897 | solution.py:46
  201.4 1.9 fusion.23
  203.6 1.1 fusion.27
  204.8 1.9 fusion.23
  207.1 1.1 fusion.27
  208.3 1.9 fusion.23
  211.7 1.9 fusion.23
  214.0 1.1 fusion.27
  215.2 1.9 fusion.23
  217.4 1.1 fusion.27
  218.7 1.9 fusion.23
  220.9 1.1 fusion.27
  222.1 1.9 fusion.23
  224.4 1.1 fusion.27
  225.6 1.9 fusion.23
  227.8 1.1 fusion.27
  229.0 1.9 fusion.23
  231.3 1.1 fusion.27
  232.5 1.9 fusion.23
  235.9 1.9 fusion.23
  238.2 1.1 fusion.27
  239.4 1.9 fusion.23
  241.6 1.1 fusion.27
  242.8 1.9 fusion.23
  246.3 1.9 fusion.23
  249.7 1.9 fusion.23
  253.2 1.9 fusion.23
  256.6 42.2 %pmax.7 = f32[256]{0:T(256)S(1)} all-reduce(f32[256]{0:T(256)S(1)} %get-tuple-element.42), channel_id=1, replica_groups=mesh['af'=8,'vert'=64] {'af'}, use_global_device_ids=true, to_apply=%region_5.6 | all-reduce | flops 256 | bytes 2048 | tf_op jit(solution)/shard_map/pmax | solution.py:69
  298.7 36.0 %all-reduce = (f32[3,256]{1,0:T(4,128)S(1)}, f32[256]{0:T(256)S(1)}) all-reduce(f32[3,256]{1,0:T(4,128)S(1)} %broadcast_multiply_fusion, f32[256]{0:T(256)S(1)} %get-tuple-element.100), channel_id=1, replica_groups=mesh['af'=8,'vert'=64] {'af'}, use_global_device_ids=true, to_apply=%region_6.7 | all-reduce | flops 1024 | bytes 8192 | tf_op jit(solution)/shard_map/psum | solution.py:71
  (102 shorter events, 16.2 us)
Async XLA Ops:
  7.2 0.8 copy-start
  7.2 191.2 %all-gather.4.cloned.1.call-start = ((), (), s32[]{:S(2)}) async-start(), calls=%async_computation | async-start | bytes 2129920 | tf_op jit(solution)/shard_map/all_gather | solution.py:65
  256.5 78.8 %copy-start.1 = (f32[10,256]{1,0:T(8,128)}, f32[10,256]{1,0:T(8,128)S(1)}, u32[]{:S(2)}) copy-start(f32[10,256]{1,0:T(8,128)S(1)} %get-tuple-element.184) | copy-start | bytes 30724
Sparse Core Ops, SparseCore 0:
  10.2 125.7 all-gather.3

commit v2 on v0

--- a/solution.py
+++ b/solution.py
@@ -63,7 +63,9 @@
         start_state(coefficients.shape[1]),
         (
             lax.all_gather(atoms, "vert", axis=1, tiled=True),
-            lax.all_gather(params, "vert", axis=1, tiled=True),
+            jnp.concatenate(
+                lax.all_to_all(jnp.stack([params] * lax.axis_size("vert")), "vert", 0, 0), axis=1
+            ),
         ),
     )
     global_peak = lax.pmax(run_peak, "af")

time: 353 us -> 281 us (0.80)
  the two profiles are of different devices: /device:TPU:2 before, /device:TPU:40 now
where the time goes in v2:
time: 281 us
  blocking collectives  153 us (54%)
  matrix products  48.2 us (17%)
  waiting for transfers between devices  37.4 us (13%)
  starting transfers between devices  15.8 us (6%)
  between operations  14.1 us (5%)
  other arithmetic  6.72 us (2%)
  local copies, waits for them, and re-layouts  5.61 us (2%)
    psum x1, blocking collectives, on_device(): coefficients = lax.psum(partial_sums, 'af')  74.5 us
    pmax x1, blocking collectives, on_device(): global_peak = lax.pmax(run_peak, 'af')  42 us
    all_gather x1, waiting for transfers between devices, on_device(): lax.all_gather(atoms, 'vert', axis=1, tiled=True)  36.7 us
    psum x1, blocking collectives, on_device(): lax.psum((run_total * factor, run_weighted * factor[None, :]), 'af')  36.1 us
    dot_general x16, matrix products, fold_block(): lax.dot_general(coefficients, atom_piece, (((0,), (0,)), ((), ())), preci...  29.7 us
    dot_general x16, matrix products, fold_block(): lax.dot_general(param_piece, weights, (((1,), (1,)), ((), ())), precision...  17.7 us
    all_to_all x1, starting transfers between devices, on_device(): lax.all_to_all(jnp.stack([params] * lax.axis_size('vert')), 'vert', 0, 0)  15.7 us
    reduce_sum x16, other arithmetic, fold_block(): run_total = run_total * factor + jnp.sum(weights, axis=1)  5.74 us
  transfers between devices with their start and end apart: 2, of which 1 were waited for; matrix products, arithmetic and copies ran while one was open for 2% of the time, Pallas kernels for 0%

profile of v2, /device:TPU:40, one launch (start us, length us, event | category | flops | bytes accessed | tf_op | source)
XLA Modules:
  0.0 281.1 jit_solution(6309764787879343850)
XLA Ops:
  7.9 1.6 stack.2
  9.5 15.7 %all-to-all-start = ((f32[64,3,512]{2,1,0:T(4,128)}), f32[64,3,512]{2,1,0:T(4,128)S(1)}, u32[]{:S(2)}, u32[]{:S(2)}) async-start(f32[64,3,512]{2,1,0:T(4,128)} %stack.2), calls=%async_computation | async-start | bytes 1048576 | tf_op jit(solution)/shard_map/all_to_all | solution.py:67
  26.1 74.5 %psum.21 = f32[10,256]{1,0:T(8,128)S(1)} all-reduce(f32[10,256]{1,0:T(8,128)S(1)} %fusion.11), channel_id=1, replica_groups=mesh['af'=8,'vert'=64] {'af'}, use_global_device_ids=true, to_apply=%region_0.0 | all-reduce | flops 2560 | bytes 20480 | tf_op jit(solution)/shard_map/psum | solution.py:60
  100.5 36.7 %all-gather.2.cloned.1.call-done = f32[10,32768]{1,0:T(8,128)} async-done(((f32[10,512]{1,0:T(8,128)}), f32[10,32768]{1,0:T(8,128)}) %all-gather.2.cloned.1.call-update) | async-done | bytes 1310736 | tf_op jit(solution)/shard_map/all_gather | solution.py:65
  137.3 2.8 copy.8
  140.2 55.3 %while.15 = (s32[]{:T(128)}, f32[256]{0:T(256)S(1)}, f32[256]{0:T(256)S(1)}, f32[3,256]{1,0:T(4,128)S(1)}, f32[16,10,2048]{2,0,1:T(8,128)S(1)}, /*index=5*/f32[1...) while((s32[]{:T(128)}, f32[256]{0:T(256)S(1)}, f32[256]{0:T(256)S(1)}, ...), condition=%wide.region_4.5_spmd.clone, body=%wide.region_1.4_spmd.clone.sunk | while | flops 84413952 | bytes 6603897 | solution.py:46
  140.3 1.9 fusion.24
  142.6 1.1 fusion.28
  143.8 1.9 fusion.24
  147.2 1.9 fusion.24
  150.7 1.9 fusion.24
  152.9 1.1 fusion.28
  154.1 1.9 fusion.24
  156.4 1.1 fusion.28
  157.6 1.9 fusion.24
  159.8 1.1 fusion.28
  161.1 1.9 fusion.24
  163.3 1.1 fusion.28
  164.5 1.9 fusion.24
  166.8 1.1 fusion.28
  168.0 1.9 fusion.24
  170.2 1.1 fusion.28
  171.4 1.9 fusion.24
  173.7 1.1 fusion.28
  174.9 1.9 fusion.24
  178.3 1.9 fusion.24
  181.8 1.9 fusion.24
  185.2 1.9 fusion.24
  188.7 1.9 fusion.24
  192.2 1.9 fusion.24
  195.5 42.0 %pmax.7 = f32[256]{0:T(256)S(1)} all-reduce(f32[256]{0:T(256)S(1)} %get-tuple-element.42), channel_id=1, replica_groups=mesh['af'=8,'vert'=64] {'af'}, use_global_device_ids=true, to_apply=%region_5.6 | all-reduce | flops 256 | bytes 2048 | tf_op jit(solution)/shard_map/pmax | solution.py:71
  237.6 36.1 %all-reduce = (f32[3,256]{1,0:T(4,128)S(1)}, f32[256]{0:T(256)S(1)}) all-reduce(f32[3,256]{1,0:T(4,128)S(1)} %broadcast_multiply_fusion, f32[256]{0:T(256)S(1)} %get-tuple-element.93), channel_id=1, replica_groups=mesh['af'=8,'vert'=64] {'af'}, use_global_device_ids=true, to_apply=%region_6.7 | all-reduce | flops 1024 | bytes 8192 | tf_op jit(solution)/shard_map/psum | solution.py:73
  (103 shorter events, 18.3 us)
Async XLA Ops:
  7.2 18.1 %copy-start = (bf16[125,256]{1,0:T(8,128)(2,1)S(1)}, bf16[125,256]{1,0:T(8,128)(2,1)}, u32[]{:S(2)}) copy-start(bf16[125,256]{1,0:T(8,128)(2,1)} %param.6) | copy-start | bytes 192004
  7.2 130.1 %all-gather.2.cloned.1.call-start = ((), (), s32[]{:S(2)}) async-start(), calls=%async_computation.1 | async-start | bytes 2129920 | tf_op jit(solution)/shard_map/all_gather | solution.py:65
  9.5 130.7 %all-to-all-start = ((f32[64,3,512]{2,1,0:T(4,128)}), f32[64,3,512]{2,1,0:T(4,128)S(1)}, u32[]{:S(2)}, u32[]{:S(2)}) async-start(f32[64,3,512]{2,1,0:T(4,128)} %stack.2), calls=%async_computation | async-start | bytes 1048576 | tf_op jit(solution)/shard_map/all_to_all | solution.py:67
  195.5 78.7 %copy-start.1 = (f32[10,256]{1,0:T(8,128)}, f32[10,256]{1,0:T(8,128)S(1)}, u32[]{:S(2)}) copy-start(f32[10,256]{1,0:T(8,128)S(1)} %get-tuple-element.178) | copy-start | bytes 30724
Sparse Core Ops, SparseCore 0:
  10.2 127.0 all-gather.1
